TPU v7x, 128 devices: a whole 4x4x4 slice. The times are simulated.
128 devices in a mesh: ctx: 32 (over z, x_hi, y), tp: 4 (over x_lo, core).
Axes of the slice: x: 4 (x_hi: 2, x_lo: 2; x = x_hi * 2 + x_lo), y: 4, z: 4, core: 2. Of those that a mesh axis runs over, the one named last changes fastest.
Arguments:
- queries: bfloat16 [16384, 4096], P('ctx', 'tp'), may hold values from -6 to 6
- keys: bfloat16 [16384, 512], P('ctx', 'tp'), may hold values from -6 to 6
- values: bfloat16 [16384, 512], P('ctx', 'tp'), may hold values from -6 to 6
- out_weight: bfloat16 [4096, 8192], P('tp'), may hold values from -0.75 to 0.75
- vertical: int32 [32, 16], P('tp'), may hold values from 0 to 255, as said below
- slash: int32 [32, 8], P('tp'), may hold values from 0 to 15, as said below
Outputs:
- projected: bfloat16 [16384, 8192], P(('ctx', 'tp'))
Inputs may be any that keep to these rules, and one draw needn't show every extreme that they name: `vertical`: each head's 16 blocks are distinct. For each index of tp, the blocks named by its 8 heads include at most 2 blocks of any one ctx shard of 512 tokens, and exactly 2 of some shard. `slash`: each head's first offset is 0 and its 8 offsets are distinct.
All inputs are finite; a program needn't handle non-finite values.
Results may differ from a plain program's by a relative error of at most 0.013.
Values may be sent and summed in bfloat16 or wider, within the bound.
A program may use at most 128 MiB of HBM per device.

v0:
```python
import jax
import jax.numpy as jnp
from jax import lax
from jax.sharding import PartitionSpec as P

HS = 128
BLK = 64


def slot_table(vert_row, slash_row, query_blocks):
    block_count = query_blocks.shape[0]
    column_ids = query_blocks[:, None]
    vert_blocks = jnp.broadcast_to(vert_row[None, :], (block_count, vert_row.shape[0]))
    vert_ok = vert_blocks <= column_ids
    slash_blocks = column_ids - slash_row[None, :]
    repeated = jnp.any(slash_blocks[:, :, None] == vert_row[None, None, :], axis=2)
    slash_ok = (slash_blocks >= 0) & jnp.logical_not(repeated)
    blocks = jnp.concatenate([vert_blocks, slash_blocks], axis=1)
    usable = jnp.concatenate([vert_ok, slash_ok], axis=1)
    return (blocks, usable)


def attend(head_query, key_tiles, value_tiles, blocks, usable, query_blocks):
    block_len = head_query.shape[1]
    score_scale = 1.0 / jnp.sqrt(jnp.float32(head_query.shape[2]))
    scores = (
        jnp.einsum("ibd,isjd->ibsj", head_query, key_tiles, preferred_element_type=jnp.float32)
        * score_scale
    )
    diagonal = blocks == query_blocks[:, None]
    positions = jnp.arange(block_len, dtype=jnp.int32)
    above_diag = positions[None, :] > positions[:, None]
    blocked = (
        jnp.logical_not(usable)[:, None, :, None]
        | diagonal[:, None, :, None] & above_diag[None, :, None, :]
    )
    scores = jnp.where(blocked, jnp.float32(-1e30), scores)
    row_max = jnp.max(scores, axis=(2, 3), keepdims=True)
    weights = jnp.exp(scores - row_max)
    row_total = jnp.sum(weights, axis=(2, 3))
    rounded_probs = weights.astype(jnp.bfloat16)
    attended = jnp.einsum(
        "ibsj,isjd->ibd", rounded_probs, value_tiles, preferred_element_type=jnp.float32
    )
    return (attended / row_total[:, :, None]).astype(jnp.bfloat16)


def shards(queries, keys, values, out_weight, vertical, slash):
    local_rows = queries.shape[0]
    local_heads = vertical.shape[0]
    local_blocks = local_rows // BLK
    ctx_rank = lax.axis_index("ctx")
    keyvals = jnp.concatenate([keys, values], axis=1).reshape(local_blocks, BLK, 2 * HS)
    first_block = ctx_rank * local_blocks
    query_blocks = first_block + jnp.arange(local_blocks, dtype=jnp.int32)
    source = lax.all_gather(keyvals, "ctx", axis=0, tiled=True)

    def locate(blocks):
        return jnp.clip(blocks, 0, source.shape[0] - 1)

    head_queries = queries.reshape(local_blocks, BLK, local_heads, HS).transpose(2, 0, 1, 3)

    def one_head(inputs):
        head_query, vert_row, slash_row = inputs
        blocks, usable = slot_table(vert_row, slash_row, query_blocks)
        chosen = source[locate(blocks)]
        return attend(head_query, chosen[..., :HS], chosen[..., HS:], blocks, usable, query_blocks)

    heads_out = lax.map(one_head, (head_queries, vertical, slash))
    attended = heads_out.transpose(1, 2, 0, 3).reshape(local_rows, local_heads * HS)
    product = jnp.dot(attended, out_weight, preferred_element_type=jnp.float32)
    return lax.psum_scatter(
        lax.optimization_barrier(product.astype(jnp.bfloat16))
        .astype(jnp.float32)
        .astype(jnp.bfloat16),
        "tp",
        scatter_dimension=0,
        tiled=True,
    )


def solution(mesh):
    return jax.shard_map(
        shards,
        mesh=mesh,
        in_specs=(
            P("ctx", "tp"),
            P("ctx", "tp"),
            P("ctx", "tp"),
            P("tp", None),
            P("tp", None),
            P("tp", None),
        ),
        out_specs=P(("ctx", "tp"), None),
        check_vma=False,
    )
```

profile of v0, /device:TPU:1, one launch (start us, length us, event | category | flops | bytes accessed | tf_op | source)
XLA Modules:
  0.0 411.1 jit_solution(11067707473191889496)
XLA Ops:
  6.5 1.7 pad_maximum_fusion
  8.3 1.5 copy.21
  9.9 0.3 copy.16
  10.2 107.0 %all-gather.2.cloned.1.call-done = bf16[256,64,256]{2,1,0:T(8,128)(2,1)} async-done(((bf16[8,64,256]{2,1,0:T(8,128)(2,1)}), bf16[256,64,256]{2,1,0:T(8,128)(2,1)}) %all-gather.2.cloned.1.call-update) | async-done | bytes 8388624 | tf_op jit(solution)/shard_map/all_gather | solution.py:56
  117.2 191.7 %while.11 = (s32[]{:T(128)}, bf16[8,8,64,128]{3,2,1,0:T(8,128)(2,1)S(1)}, s32[8,16]{1,0:T(8,128)}, s32[8,8]{1,0:T(8,128)}, bf16[8,8,64,128]{3,2,1,0:T(8,128)(2,1...) while((s32[]{:T(128)}, bf16[8,8,64,128]{3,2,1,0:T(8,128)(2,1)S(1)}, ...), condition=%wide.region_4.5_spmd.clone, body=%wide.region_0.4_spmd.clone.sunk | while | flops 416161856 | bytes 50649856 | solution.py:69
  117.2 0.7 fusion.59
  118.0 0.7 fusion.60
  118.7 0.3 compare_reduce_fusion.2
  119.4 11.5 %gather_fusion = bf16[192,64,256]{2,1,0:T(8,128)(2,1)} fusion(bf16[256,64,256]{2,1,0:T(8,128)(2,1)} %get-tuple-element.179, s32[1024]{0:T(1024)S(1)} %pad_clamp_fusion.2), kind=kCustom, calls=%fused_computation.clone.clone.1 | custom fusion | bytes 12583680 | tf_op jit(solution)/shard_map/while/body/eval_jaxpr/gather | solution.py:66
  130.9 4.4 %fusion.61 = (f32[8,64]{1,0:T(8,128)S(1)}, f32[8,64,24,64]{1,3,2,0:T(8,128)S(1)}) fusion(pred[64,64]{0,1:T(8,128)(4,1)S(1)} %iota_compare_fusion.2, pred[8,24]{1,0:T(8,128)(4,1)S(1)} %get-tuple-element.152, pred[8,24]{1,0:T(8,128)(4,1)S(1)} %get-tuple-element.153, bf16[8,24,64,256]{3,2,1,0:T(8,128)(2,1)} %bitcast.59, ...), kind=kOutput, calls=%fused_computation.6.clone.1 | convolution fusion | flops 205258240 | bytes 6435328 | tf_op jit(solution)/shard_map/while/body/eval_jaxpr/ibd,isjd->ibsj/dot_general | solution.py:27
  135.3 2.5 fusion.62
  137.8 3.4 fusion.63
  141.2 0.7 fusion.59
  141.9 0.7 fusion.60
  142.6 0.3 compare_reduce_fusion.2
  143.3 11.5 %gather_fusion = bf16[192,64,256]{2,1,0:T(8,128)(2,1)} fusion(bf16[256,64,256]{2,1,0:T(8,128)(2,1)} %get-tuple-element.179, s32[1024]{0:T(1024)S(1)} %pad_clamp_fusion.2), kind=kCustom, calls=%fused_computation.clone.clone.1 | custom fusion | bytes 12583680 | tf_op jit(solution)/shard_map/while/body/eval_jaxpr/gather | solution.py:66
  154.8 4.4 %fusion.61 = (f32[8,64]{1,0:T(8,128)S(1)}, f32[8,64,24,64]{1,3,2,0:T(8,128)S(1)}) fusion(pred[64,64]{0,1:T(8,128)(4,1)S(1)} %iota_compare_fusion.2, pred[8,24]{1,0:T(8,128)(4,1)S(1)} %get-tuple-element.152, pred[8,24]{1,0:T(8,128)(4,1)S(1)} %get-tuple-element.153, bf16[8,24,64,256]{3,2,1,0:T(8,128)(2,1)} %bitcast.59, ...), kind=kOutput, calls=%fused_computation.6.clone.1 | convolution fusion | flops 205258240 | bytes 6435328 | tf_op jit(solution)/shard_map/while/body/eval_jaxpr/ibd,isjd->ibsj/dot_general | solution.py:27
  159.2 2.5 fusion.62
  161.7 3.4 fusion.63
  165.1 0.7 fusion.59
  165.9 0.7 fusion.60
  166.6 0.3 compare_reduce_fusion.2
  167.3 11.5 %gather_fusion = bf16[192,64,256]{2,1,0:T(8,128)(2,1)} fusion(bf16[256,64,256]{2,1,0:T(8,128)(2,1)} %get-tuple-element.179, s32[1024]{0:T(1024)S(1)} %pad_clamp_fusion.2), kind=kCustom, calls=%fused_computation.clone.clone.1 | custom fusion | bytes 12583680 | tf_op jit(solution)/shard_map/while/body/eval_jaxpr/gather | solution.py:66
  178.8 4.4 %fusion.61 = (f32[8,64]{1,0:T(8,128)S(1)}, f32[8,64,24,64]{1,3,2,0:T(8,128)S(1)}) fusion(pred[64,64]{0,1:T(8,128)(4,1)S(1)} %iota_compare_fusion.2, pred[8,24]{1,0:T(8,128)(4,1)S(1)} %get-tuple-element.152, pred[8,24]{1,0:T(8,128)(4,1)S(1)} %get-tuple-element.153, bf16[8,24,64,256]{3,2,1,0:T(8,128)(2,1)} %bitcast.59, ...), kind=kOutput, calls=%fused_computation.6.clone.1 | convolution fusion | flops 205258240 | bytes 6435328 | tf_op jit(solution)/shard_map/while/body/eval_jaxpr/ibd,isjd->ibsj/dot_general | solution.py:27
  183.2 2.5 fusion.62
  185.7 3.4 fusion.63
  189.1 0.7 fusion.59
  189.9 0.7 fusion.60
  190.5 0.3 compare_reduce_fusion.2
  191.2 11.5 %gather_fusion = bf16[192,64,256]{2,1,0:T(8,128)(2,1)} fusion(bf16[256,64,256]{2,1,0:T(8,128)(2,1)} %get-tuple-element.179, s32[1024]{0:T(1024)S(1)} %pad_clamp_fusion.2), kind=kCustom, calls=%fused_computation.clone.clone.1 | custom fusion | bytes 12583680 | tf_op jit(solution)/shard_map/while/body/eval_jaxpr/gather | solution.py:66
  202.8 4.4 %fusion.61 = (f32[8,64]{1,0:T(8,128)S(1)}, f32[8,64,24,64]{1,3,2,0:T(8,128)S(1)}) fusion(pred[64,64]{0,1:T(8,128)(4,1)S(1)} %iota_compare_fusion.2, pred[8,24]{1,0:T(8,128)(4,1)S(1)} %get-tuple-element.152, pred[8,24]{1,0:T(8,128)(4,1)S(1)} %get-tuple-element.153, bf16[8,24,64,256]{3,2,1,0:T(8,128)(2,1)} %bitcast.59, ...), kind=kOutput, calls=%fused_computation.6.clone.1 | convolution fusion | flops 205258240 | bytes 6435328 | tf_op jit(solution)/shard_map/while/body/eval_jaxpr/ibd,isjd->ibsj/dot_general | solution.py:27
  207.2 2.5 fusion.62
  209.7 3.4 fusion.63
  213.0 0.7 fusion.59
  213.8 0.7 fusion.60
  214.5 0.3 compare_reduce_fusion.2
  215.2 11.5 %gather_fusion = bf16[192,64,256]{2,1,0:T(8,128)(2,1)} fusion(bf16[256,64,256]{2,1,0:T(8,128)(2,1)} %get-tuple-element.179, s32[1024]{0:T(1024)S(1)} %pad_clamp_fusion.2), kind=kCustom, calls=%fused_computation.clone.clone.1 | custom fusion | bytes 12583680 | tf_op jit(solution)/shard_map/while/body/eval_jaxpr/gather | solution.py:66
  226.7 4.4 %fusion.61 = (f32[8,64]{1,0:T(8,128)S(1)}, f32[8,64,24,64]{1,3,2,0:T(8,128)S(1)}) fusion(pred[64,64]{0,1:T(8,128)(4,1)S(1)} %iota_compare_fusion.2, pred[8,24]{1,0:T(8,128)(4,1)S(1)} %get-tuple-element.152, pred[8,24]{1,0:T(8,128)(4,1)S(1)} %get-tuple-element.153, bf16[8,24,64,256]{3,2,1,0:T(8,128)(2,1)} %bitcast.59, ...), kind=kOutput, calls=%fused_computation.6.clone.1 | convolution fusion | flops 205258240 | bytes 6435328 | tf_op jit(solution)/shard_map/while/body/eval_jaxpr/ibd,isjd->ibsj/dot_general | solution.py:27
  231.1 2.5 fusion.62
  233.6 3.4 fusion.63
  237.0 0.7 fusion.59
  237.8 0.7 fusion.60
  238.5 0.3 compare_reduce_fusion.2
  239.2 11.5 %gather_fusion = bf16[192,64,256]{2,1,0:T(8,128)(2,1)} fusion(bf16[256,64,256]{2,1,0:T(8,128)(2,1)} %get-tuple-element.179, s32[1024]{0:T(1024)S(1)} %pad_clamp_fusion.2), kind=kCustom, calls=%fused_computation.clone.clone.1 | custom fusion | bytes 12583680 | tf_op jit(solution)/shard_map/while/body/eval_jaxpr/gather | solution.py:66
  250.7 4.4 %fusion.61 = (f32[8,64]{1,0:T(8,128)S(1)}, f32[8,64,24,64]{1,3,2,0:T(8,128)S(1)}) fusion(pred[64,64]{0,1:T(8,128)(4,1)S(1)} %iota_compare_fusion.2, pred[8,24]{1,0:T(8,128)(4,1)S(1)} %get-tuple-element.152, pred[8,24]{1,0:T(8,128)(4,1)S(1)} %get-tuple-element.153, bf16[8,24,64,256]{3,2,1,0:T(8,128)(2,1)} %bitcast.59, ...), kind=kOutput, calls=%fused_computation.6.clone.1 | convolution fusion | flops 205258240 | bytes 6435328 | tf_op jit(solution)/shard_map/while/body/eval_jaxpr/ibd,isjd->ibsj/dot_general | solution.py:27
  255.1 2.5 fusion.62
  257.6 3.4 fusion.63
  261.0 0.7 fusion.59
  261.7 0.7 fusion.60
  262.4 0.3 compare_reduce_fusion.2
  263.1 11.5 %gather_fusion = bf16[192,64,256]{2,1,0:T(8,128)(2,1)} fusion(bf16[256,64,256]{2,1,0:T(8,128)(2,1)} %get-tuple-element.179, s32[1024]{0:T(1024)S(1)} %pad_clamp_fusion.2), kind=kCustom, calls=%fused_computation.clone.clone.1 | custom fusion | bytes 12583680 | tf_op jit(solution)/shard_map/while/body/eval_jaxpr/gather | solution.py:66
  274.6 4.4 %fusion.61 = (f32[8,64]{1,0:T(8,128)S(1)}, f32[8,64,24,64]{1,3,2,0:T(8,128)S(1)}) fusion(pred[64,64]{0,1:T(8,128)(4,1)S(1)} %iota_compare_fusion.2, pred[8,24]{1,0:T(8,128)(4,1)S(1)} %get-tuple-element.152, pred[8,24]{1,0:T(8,128)(4,1)S(1)} %get-tuple-element.153, bf16[8,24,64,256]{3,2,1,0:T(8,128)(2,1)} %bitcast.59, ...), kind=kOutput, calls=%fused_computation.6.clone.1 | convolution fusion | flops 205258240 | bytes 6435328 | tf_op jit(solution)/shard_map/while/body/eval_jaxpr/ibd,isjd->ibsj/dot_general | solution.py:27
  279.0 2.5 fusion.62
  281.5 3.4 fusion.63
  284.9 0.7 fusion.59
  285.7 0.7 fusion.60
  286.4 0.3 compare_reduce_fusion.2
  287.1 11.5 %gather_fusion = bf16[192,64,256]{2,1,0:T(8,128)(2,1)} fusion(bf16[256,64,256]{2,1,0:T(8,128)(2,1)} %get-tuple-element.179, s32[1024]{0:T(1024)S(1)} %pad_clamp_fusion.2), kind=kCustom, calls=%fused_computation.clone.clone.1 | custom fusion | bytes 12583680 | tf_op jit(solution)/shard_map/while/body/eval_jaxpr/gather | solution.py:66
  298.6 4.4 %fusion.61 = (f32[8,64]{1,0:T(8,128)S(1)}, f32[8,64,24,64]{1,3,2,0:T(8,128)S(1)}) fusion(pred[64,64]{0,1:T(8,128)(4,1)S(1)} %iota_compare_fusion.2, pred[8,24]{1,0:T(8,128)(4,1)S(1)} %get-tuple-element.152, pred[8,24]{1,0:T(8,128)(4,1)S(1)} %get-tuple-element.153, bf16[8,24,64,256]{3,2,1,0:T(8,128)(2,1)} %bitcast.59, ...), kind=kOutput, calls=%fused_computation.6.clone.1 | convolution fusion | flops 205258240 | bytes 6435328 | tf_op jit(solution)/shard_map/while/body/eval_jaxpr/ibd,isjd->ibsj/dot_general | solution.py:27
  303.0 2.5 fusion.62
  305.5 3.4 fusion.63
  308.9 0.7 copy.17
  309.6 16.8 %convolution_convert_fusion = bf16[512,8192]{1,0:T(8,128)(2,1)} fusion(bf16[1024,8192]{1,0:T(8,128)(2,1)} %param.11, bf16[64,8,8,128]{3,2,1,0:T(8,128)(2,1)S(1)} %bitcast.66), kind=kOutput, calls=%fused_computation.42 | convolution fusion | flops 8594128896 | bytes 26214400 | tf_op jit(solution)/shard_map/dot_general | solution.py:71
  326.4 77.8 %reduce-scatter.2.cloned.1.call-done = bf16[128,8192]{1,0:T(8,128)(2,1)} async-done(((bf16[512,8192]{1,0:T(8,128)(2,1)}), bf16[128,8192]{1,0:T(8,128)(2,1)}) %reduce-scatter.2.cloned.1.call-update) | async-done | bytes 2097168 | tf_op jit(solution)/shard_map/reduce_scatter | solution.py:72
  (134 shorter events, 4.2 us)
Async XLA Ops:
  6.5 110.7 %all-gather.2.cloned.1.call-start = ((), (), s32[]{:S(2)}) async-start(), calls=%async_computation.1 | async-start | bytes 8650752 | tf_op jit(solution)/shard_map/all_gather | solution.py:56
  8.3 396.0 %reduce-scatter.2.cloned.1.call-start = ((), (), s32[]{:S(2)}) async-start(), calls=%async_computation.2 | async-start | bytes 10485760 | tf_op jit(solution)/shard_map/reduce_scatter | solution.py:72
  130.9 6.9 %slice-start = ((s8[6291456]{0:T(1024)(128)(4,1)}), s8[4194304]{0:T(1024)(128)(4,1)S(1)}, s32[]{:S(2)}) async-start(s8[6291456]{0:T(1024)(128)(4,1)} %bitcast.60), calls=%async_computation.3 | async-start | bytes 8388608 | tf_op jit(solution)/shard_map/while
  130.9 6.9 %slice-start.1 = ((s8[6291456]{0:T(1024)(128)(4,1)}), s8[2097152]{0:T(1024)(128)(4,1)S(1)}, s32[]{:S(2)}) async-start(s8[6291456]{0:T(1024)(128)(4,1)} %bitcast.60), calls=%async_computation.4 | async-start | bytes 4194304 | tf_op jit(solution)/shard_map/while
  154.8 6.9 %slice-start = ((s8[6291456]{0:T(1024)(128)(4,1)}), s8[4194304]{0:T(1024)(128)(4,1)S(1)}, s32[]{:S(2)}) async-start(s8[6291456]{0:T(1024)(128)(4,1)} %bitcast.60), calls=%async_computation.3 | async-start | bytes 8388608 | tf_op jit(solution)/shard_map/while
  154.8 6.9 %slice-start.1 = ((s8[6291456]{0:T(1024)(128)(4,1)}), s8[2097152]{0:T(1024)(128)(4,1)S(1)}, s32[]{:S(2)}) async-start(s8[6291456]{0:T(1024)(128)(4,1)} %bitcast.60), calls=%async_computation.4 | async-start | bytes 4194304 | tf_op jit(solution)/shard_map/while
  178.8 6.9 %slice-start = ((s8[6291456]{0:T(1024)(128)(4,1)}), s8[4194304]{0:T(1024)(128)(4,1)S(1)}, s32[]{:S(2)}) async-start(s8[6291456]{0:T(1024)(128)(4,1)} %bitcast.60), calls=%async_computation.3 | async-start | bytes 8388608 | tf_op jit(solution)/shard_map/while
  178.8 6.9 %slice-start.1 = ((s8[6291456]{0:T(1024)(128)(4,1)}), s8[2097152]{0:T(1024)(128)(4,1)S(1)}, s32[]{:S(2)}) async-start(s8[6291456]{0:T(1024)(128)(4,1)} %bitcast.60), calls=%async_computation.4 | async-start | bytes 4194304 | tf_op jit(solution)/shard_map/while
  202.7 6.9 %slice-start = ((s8[6291456]{0:T(1024)(128)(4,1)}), s8[4194304]{0:T(1024)(128)(4,1)S(1)}, s32[]{:S(2)}) async-start(s8[6291456]{0:T(1024)(128)(4,1)} %bitcast.60), calls=%async_computation.3 | async-start | bytes 8388608 | tf_op jit(solution)/shard_map/while
  202.8 6.9 %slice-start.1 = ((s8[6291456]{0:T(1024)(128)(4,1)}), s8[2097152]{0:T(1024)(128)(4,1)S(1)}, s32[]{:S(2)}) async-start(s8[6291456]{0:T(1024)(128)(4,1)} %bitcast.60), calls=%async_computation.4 | async-start | bytes 4194304 | tf_op jit(solution)/shard_map/while
  226.7 6.9 %slice-start = ((s8[6291456]{0:T(1024)(128)(4,1)}), s8[4194304]{0:T(1024)(128)(4,1)S(1)}, s32[]{:S(2)}) async-start(s8[6291456]{0:T(1024)(128)(4,1)} %bitcast.60), calls=%async_computation.3 | async-start | bytes 8388608 | tf_op jit(solution)/shard_map/while
  226.7 6.9 %slice-start.1 = ((s8[6291456]{0:T(1024)(128)(4,1)}), s8[2097152]{0:T(1024)(128)(4,1)S(1)}, s32[]{:S(2)}) async-start(s8[6291456]{0:T(1024)(128)(4,1)} %bitcast.60), calls=%async_computation.4 | async-start | bytes 4194304 | tf_op jit(solution)/shard_map/while
  250.7 6.9 %slice-start = ((s8[6291456]{0:T(1024)(128)(4,1)}), s8[4194304]{0:T(1024)(128)(4,1)S(1)}, s32[]{:S(2)}) async-start(s8[6291456]{0:T(1024)(128)(4,1)} %bitcast.60), calls=%async_computation.3 | async-start | bytes 8388608 | tf_op jit(solution)/shard_map/while
  250.7 6.9 %slice-start.1 = ((s8[6291456]{0:T(1024)(128)(4,1)}), s8[2097152]{0:T(1024)(128)(4,1)S(1)}, s32[]{:S(2)}) async-start(s8[6291456]{0:T(1024)(128)(4,1)} %bitcast.60), calls=%async_computation.4 | async-start | bytes 4194304 | tf_op jit(solution)/shard_map/while
  274.6 6.9 %slice-start = ((s8[6291456]{0:T(1024)(128)(4,1)}), s8[4194304]{0:T(1024)(128)(4,1)S(1)}, s32[]{:S(2)}) async-start(s8[6291456]{0:T(1024)(128)(4,1)} %bitcast.60), calls=%async_computation.3 | async-start | bytes 8388608 | tf_op jit(solution)/shard_map/while
  274.6 6.9 %slice-start.1 = ((s8[6291456]{0:T(1024)(128)(4,1)}), s8[2097152]{0:T(1024)(128)(4,1)S(1)}, s32[]{:S(2)}) async-start(s8[6291456]{0:T(1024)(128)(4,1)} %bitcast.60), calls=%async_computation.4 | async-start | bytes 4194304 | tf_op jit(solution)/shard_map/while
  298.6 6.9 %slice-start = ((s8[6291456]{0:T(1024)(128)(4,1)}), s8[4194304]{0:T(1024)(128)(4,1)S(1)}, s32[]{:S(2)}) async-start(s8[6291456]{0:T(1024)(128)(4,1)} %bitcast.60), calls=%async_computation.3 | async-start | bytes 8388608 | tf_op jit(solution)/shard_map/while
  298.6 6.9 %slice-start.1 = ((s8[6291456]{0:T(1024)(128)(4,1)}), s8[2097152]{0:T(1024)(128)(4,1)S(1)}, s32[]{:S(2)}) async-start(s8[6291456]{0:T(1024)(128)(4,1)} %bitcast.60), calls=%async_computation.4 | async-start | bytes 4194304 | tf_op jit(solution)/shard_map/while
Sparse Core Ops, SparseCore 0:
  10.5 106.6 all-gather.1
  326.6 77.6 reduce-scatter.1
where the time goes:
time: 412 us; the launch traced here: 411 us
  waiting for transfers between devices  185 us (45%)
  local copies, waits for them, and re-layouts  106 us (26%)
  matrix products  78.7 us (19%)
  other arithmetic  27 us (7%)
  between operations  13.5 us (3%)
    all_gather x1, waiting for transfers between devices, shards(): source = lax.all_gather(keyvals, 'ctx', axis=0, tiled=True)  107 us
    gather x8, local copies, waits for them, and re-layouts, one_head(): chosen = source[locate(blocks)]  91.8 us
    reduce_scatter x1, waiting for transfers between devices, shards(): lax.psum_scatter(lax.optimization_barrier(product.astype(jnp.bfloat16)).a...  77.8 us
    dot_general x8, matrix products, attend(): jnp.einsum('ibd,isjd->ibsj', head_query, key_tiles, preferred_element_typ...  35.1 us
    dot_general x8, matrix products, attend(): jnp.einsum('ibsj,isjd->ibd', rounded_probs, value_tiles, preferred_elemen...  26.8 us
    reduce_sum x8, other arithmetic, attend(): row_total = jnp.sum(weights, axis=(2, 3))  19.8 us
    dot_general x1, matrix products, shards(): product = jnp.dot(attended, out_weight, preferred_element_type=jnp.float32)  16.8 us
  transfers between devices with their start and end apart: 2, of which 2 were waited for; matrix products, arithmetic and copies ran while one was open for 0% of the time, Pallas kernels for 0%

commit v1 on v0

--- a/solution.py
+++ b/solution.py
@@ -53,7 +53,16 @@
     keyvals = jnp.concatenate([keys, values], axis=1).reshape(local_blocks, BLK, 2 * HS)
     first_block = ctx_rank * local_blocks
     query_blocks = first_block + jnp.arange(local_blocks, dtype=jnp.int32)
-    source = lax.all_gather(keyvals, "ctx", axis=0, tiled=True)
+    spread_stages_all = lambda u_in, which_axis, along_dim: jnp.concatenate(
+        lax.all_to_all(
+            jnp.stack([u_in for _ in range(lax.axis_size(which_axis))]),
+            axis_name=which_axis,
+            split_axis=0,
+            concat_axis=0,
+        ),
+        axis=along_dim,
+    )
+    source = spread_stages_all(keyvals, "ctx", 0)
 
     def locate(blocks):
         return jnp.clip(blocks, 0, source.shape[0] - 1)

time: 412 us -> 446 us (1.083)
  waiting for transfers between devices: 185 us -> 205 us
  starting transfers between devices: 0.04 us -> 11.6 us
    all_to_all x0 -> x1, waiting for transfers between devices: none -> 111 us  [shards(): lax.all_to_all(jnp.stack([u_in for _ in range(lax.axis_size(which_axis))]...]
    all_gather x1 -> x0, waiting for transfers between devices: 107 us -> none  [shards(): source = lax.all_gather(keyvals, 'ctx', axis=0, tiled=True)]
    reduce_scatter x1, waiting for transfers between devices: 77.8 us -> 93.8 us  [shards(): lax.psum_scatter(lax.optimization_barrier(product.astype(jnp.bfloat16)).a...]
    all_to_all x0 -> x1, starting transfers between devices: none -> 11.6 us  [shards(): lax.all_to_all(jnp.stack([u_in for _ in range(lax.axis_size(which_axis))]...]
where the time goes in v1:
time: 446 us; the launch traced here: 445 us
  waiting for transfers between devices  205 us (46%)
  local copies, waits for them, and re-layouts  109 us (24%)
  matrix products  78.8 us (18%)
  other arithmetic  26.3 us (6%)
  between operations  13.5 us (3%)
  starting transfers between devices  11.6 us (3%)
    all_to_all x1, waiting for transfers between devices, shards(): lax.all_to_all(jnp.stack([u_in for _ in range(lax.axis_size(which_axis))]...  111 us
    reduce_scatter x1, waiting for transfers between devices, shards(): lax.psum_scatter(lax.optimization_barrier(product.astype(jnp.bfloat16)).a...  93.8 us
    gather x8, local copies, waits for them, and re-layouts, one_head(): chosen = source[locate(blocks)]  91.8 us
    dot_general x8, matrix products, attend(): jnp.einsum('ibd,isjd->ibsj', head_query, key_tiles, preferred_element_typ...  35.1 us
    dot_general x8, matrix products, attend(): jnp.einsum('ibsj,isjd->ibd', rounded_probs, value_tiles, preferred_elemen...  26.8 us
    reduce_sum x8, other arithmetic, attend(): row_total = jnp.sum(weights, axis=(2, 3))  19.8 us
    dot_general x1, matrix products, shards(): product = jnp.dot(attended, out_weight, preferred_element_type=jnp.float32)  16.8 us
    all_to_all x1, starting transfers between devices, shards(): lax.all_to_all(jnp.stack([u_in for _ in range(lax.axis_size(which_axis))]...  11.6 us
  transfers between devices with their start and end apart: 2, of which 2 were waited for; matrix products, arithmetic and copies ran while one was open for 0% of the time, Pallas kernels for 0%

profile of v1, /device:TPU:1, one launch (start us, length us, event | category | flops | bytes accessed | tf_op | source)
XLA Modules:
  0.0 444.8 jit_solution(235820959232807907)
XLA Ops:
  6.5 1.0 pad_maximum_fusion
  7.5 4.3 stack.3
  11.8 11.6 %all-to-all-start = ((bf16[32,8,64,256]{3,2,1,0:T(8,128)(2,1)}), bf16[32,8,64,256]{3,2,1,0:T(8,128)(2,1)}, u32[]{:S(2)}, u32[]{:S(2)}) async-start(bf16[32,8,64,256]{3,2,1,0:T(8,128)(2,1)} %stack.3), calls=%async_computation | async-start | bytes 16777216 | tf_op jit(solution)/shard_map/all_to_all | solution.py:57
  24.1 110.8 %all-to-all-done = bf16[32,8,64,256]{3,2,1,0:T(8,128)(2,1)} async-done(((bf16[32,8,64,256]{3,2,1,0:T(8,128)(2,1)}), bf16[32,8,64,256]{3,2,1,0:T(8,128)(2,1)}, u32[]{:S(2)}, u32[]{:S(2)}) %all-to-all-start) | async-done | bytes 8388640 | tf_op jit(solution)/shard_map/all_to_all | solution.py:57
  135.0 191.7 %while.11 = (s32[]{:T(128)}, bf16[8,8,64,128]{3,2,1,0:T(8,128)(2,1)S(1)}, s32[8,16]{1,0:T(8,128)}, s32[8,8]{1,0:T(8,128)}, bf16[8,8,64,128]{3,2,1,0:T(8,128)(2,1...) while((s32[]{:T(128)}, bf16[8,8,64,128]{3,2,1,0:T(8,128)(2,1)S(1)}, ...), condition=%wide.region_4.5_spmd.clone, body=%wide.region_0.4_spmd.clone.sunk | while | flops 416161856 | bytes 50649856 | solution.py:78
  135.0 0.7 fusion.59
  135.7 0.7 fusion.60
  136.4 0.3 compare_reduce_fusion.2
  137.1 11.5 %gather_fusion = bf16[192,64,256]{2,1,0:T(8,128)(2,1)} fusion(bf16[256,64,256]{2,1,0:T(8,128)(2,1)} %get-tuple-element.172, s32[1024]{0:T(1024)S(1)} %pad_clamp_fusion.2), kind=kCustom, calls=%fused_computation.clone.clone.1 | custom fusion | bytes 12583680 | tf_op jit(solution)/shard_map/while/body/eval_jaxpr/gather | solution.py:75
  148.6 4.4 fusion.61
  153.0 2.5 fusion.62
  155.5 3.4 fusion.63
  158.9 0.7 fusion.59
  159.7 0.7 fusion.60
  160.4 0.3 compare_reduce_fusion.2
  161.1 11.5 %gather_fusion = bf16[192,64,256]{2,1,0:T(8,128)(2,1)} fusion(bf16[256,64,256]{2,1,0:T(8,128)(2,1)} %get-tuple-element.172, s32[1024]{0:T(1024)S(1)} %pad_clamp_fusion.2), kind=kCustom, calls=%fused_computation.clone.clone.1 | custom fusion | bytes 12583680 | tf_op jit(solution)/shard_map/while/body/eval_jaxpr/gather | solution.py:75
  172.6 4.4 fusion.61
  177.0 2.5 fusion.62
  179.5 3.4 fusion.63
  182.9 0.7 fusion.59
  183.7 0.7 fusion.60
  184.3 0.3 compare_reduce_fusion.2
  185.1 11.5 %gather_fusion = bf16[192,64,256]{2,1,0:T(8,128)(2,1)} fusion(bf16[256,64,256]{2,1,0:T(8,128)(2,1)} %get-tuple-element.172, s32[1024]{0:T(1024)S(1)} %pad_clamp_fusion.2), kind=kCustom, calls=%fused_computation.clone.clone.1 | custom fusion | bytes 12583680 | tf_op jit(solution)/shard_map/while/body/eval_jaxpr/gather | solution.py:75
  196.6 4.4 fusion.61
  201.0 2.5 fusion.62
  203.5 3.4 fusion.63
  206.8 0.7 fusion.59
  207.6 0.7 fusion.60
  208.3 0.3 compare_reduce_fusion.2
  209.0 11.5 %gather_fusion = bf16[192,64,256]{2,1,0:T(8,128)(2,1)} fusion(bf16[256,64,256]{2,1,0:T(8,128)(2,1)} %get-tuple-element.172, s32[1024]{0:T(1024)S(1)} %pad_clamp_fusion.2), kind=kCustom, calls=%fused_computation.clone.clone.1 | custom fusion | bytes 12583680 | tf_op jit(solution)/shard_map/while/body/eval_jaxpr/gather | solution.py:75
  220.5 4.4 fusion.61
  224.9 2.5 fusion.62
  227.4 3.4 fusion.63
  230.8 0.7 fusion.59
  231.6 0.7 fusion.60
  232.3 0.3 compare_reduce_fusion.2
  233.0 11.5 %gather_fusion = bf16[192,64,256]{2,1,0:T(8,128)(2,1)} fusion(bf16[256,64,256]{2,1,0:T(8,128)(2,1)} %get-tuple-element.172, s32[1024]{0:T(1024)S(1)} %pad_clamp_fusion.2), kind=kCustom, calls=%fused_computation.clone.clone.1 | custom fusion | bytes 12583680 | tf_op jit(solution)/shard_map/while/body/eval_jaxpr/gather | solution.py:75
  244.5 4.4 fusion.61
  248.9 2.5 fusion.62
  251.4 3.4 fusion.63
  254.8 0.7 fusion.59
  255.5 0.7 fusion.60
  256.2 0.3 compare_reduce_fusion.2
  256.9 11.5 %gather_fusion = bf16[192,64,256]{2,1,0:T(8,128)(2,1)} fusion(bf16[256,64,256]{2,1,0:T(8,128)(2,1)} %get-tuple-element.172, s32[1024]{0:T(1024)S(1)} %pad_clamp_fusion.2), kind=kCustom, calls=%fused_computation.clone.clone.1 | custom fusion | bytes 12583680 | tf_op jit(solution)/shard_map/while/body/eval_jaxpr/gather | solution.py:75
  268.4 4.4 fusion.61
  272.8 2.5 fusion.62
  275.3 3.4 fusion.63
  278.7 0.7 fusion.59
  279.5 0.7 fusion.60
  280.2 0.3 compare_reduce_fusion.2
  280.9 11.5 %gather_fusion = bf16[192,64,256]{2,1,0:T(8,128)(2,1)} fusion(bf16[256,64,256]{2,1,0:T(8,128)(2,1)} %get-tuple-element.172, s32[1024]{0:T(1024)S(1)} %pad_clamp_fusion.2), kind=kCustom, calls=%fused_computation.clone.clone.1 | custom fusion | bytes 12583680 | tf_op jit(solution)/shard_map/while/body/eval_jaxpr/gather | solution.py:75
  292.4 4.4 fusion.61
  296.8 2.5 fusion.62
  299.3 3.4 fusion.63
  302.7 0.7 fusion.59
  303.5 0.7 fusion.60
  304.2 0.3 compare_reduce_fusion.2
  304.9 11.5 %gather_fusion = bf16[192,64,256]{2,1,0:T(8,128)(2,1)} fusion(bf16[256,64,256]{2,1,0:T(8,128)(2,1)} %get-tuple-element.172, s32[1024]{0:T(1024)S(1)} %pad_clamp_fusion.2), kind=kCustom, calls=%fused_computation.clone.clone.1 | custom fusion | bytes 12583680 | tf_op jit(solution)/shard_map/while/body/eval_jaxpr/gather | solution.py:75
  316.4 4.4 fusion.61
  320.8 2.5 fusion.62
  323.3 3.4 fusion.63
  326.6 0.7 copy.14
  327.3 16.8 %convolution_convert_fusion = bf16[512,8192]{1,0:T(8,128)(2,1)} fusion(bf16[1024,8192]{1,0:T(8,128)(2,1)} %param.11, bf16[64,8,8,128]{3,2,1,0:T(8,128)(2,1)S(1)} %bitcast.68), kind=kOutput, calls=%fused_computation.42 | convolution fusion | flops 8594128896 | bytes 26214400 | tf_op jit(solution)/shard_map/dot_general | solution.py:80
  344.2 93.8 %reduce-scatter.2.cloned.1.call-done = bf16[128,8192]{1,0:T(8,128)(2,1)} async-done(((bf16[512,8192]{1,0:T(8,128)(2,1)}), bf16[128,8192]{1,0:T(8,128)(2,1)}) %reduce-scatter.2.cloned.1.call-update) | async-done | bytes 2097168 | tf_op jit(solution)/shard_map/reduce_scatter | solution.py:81
  (136 shorter events, 4.7 us)
Async XLA Ops:
  11.8 11.7 %copy-start = (bf16[512,1024]{1,0:T(8,128)(2,1)S(1)}, bf16[512,1024]{1,0:T(8,128)(2,1)}, u32[]{:S(2)}) copy-start(bf16[512,1024]{1,0:T(8,128)(2,1)} %param.8) | copy-start | bytes 3145732
  11.8 123.1 %all-to-all-start = ((bf16[32,8,64,256]{3,2,1,0:T(8,128)(2,1)}), bf16[32,8,64,256]{3,2,1,0:T(8,128)(2,1)}, u32[]{:S(2)}, u32[]{:S(2)}) async-start(bf16[32,8,64,256]{3,2,1,0:T(8,128)(2,1)} %stack.3), calls=%async_computation | async-start | bytes 16777216 | tf_op jit(solution)/shard_map/all_to_all | solution.py:57
  23.4 414.5 %reduce-scatter.2.cloned.1.call-start = ((), (), s32[]{:S(2)}) async-start(), calls=%async_computation.2 | async-start | bytes 10485760 | tf_op jit(solution)/shard_map/reduce_scatter | solution.py:81
  148.6 6.9 %slice-start = ((s8[6291456]{0:T(1024)(128)(4,1)}), s8[4194304]{0:T(1024)(128)(4,1)S(1)}, s32[]{:S(2)}) async-start(s8[6291456]{0:T(1024)(128)(4,1)} %bitcast.61), calls=%async_computation.3 | async-start | bytes 8388608 | tf_op jit(solution)/shard_map/while
  148.6 6.9 %slice-start.1 = ((s8[6291456]{0:T(1024)(128)(4,1)}), s8[2097152]{0:T(1024)(128)(4,1)S(1)}, s32[]{:S(2)}) async-start(s8[6291456]{0:T(1024)(128)(4,1)} %bitcast.61), calls=%async_computation.4 | async-start | bytes 4194304 | tf_op jit(solution)/shard_map/while
  172.6 6.9 %slice-start = ((s8[6291456]{0:T(1024)(128)(4,1)}), s8[4194304]{0:T(1024)(128)(4,1)S(1)}, s32[]{:S(2)}) async-start(s8[6291456]{0:T(1024)(128)(4,1)} %bitcast.61), calls=%async_computation.3 | async-start | bytes 8388608 | tf_op jit(solution)/shard_map/while
  172.6 6.9 %slice-start.1 = ((s8[6291456]{0:T(1024)(128)(4,1)}), s8[2097152]{0:T(1024)(128)(4,1)S(1)}, s32[]{:S(2)}) async-start(s8[6291456]{0:T(1024)(128)(4,1)} %bitcast.61), calls=%async_computation.4 | async-start | bytes 4194304 | tf_op jit(solution)/shard_map/while
  196.5 6.9 %slice-start = ((s8[6291456]{0:T(1024)(128)(4,1)}), s8[4194304]{0:T(1024)(128)(4,1)S(1)}, s32[]{:S(2)}) async-start(s8[6291456]{0:T(1024)(128)(4,1)} %bitcast.61), calls=%async_computation.3 | async-start | bytes 8388608 | tf_op jit(solution)/shard_map/while
  196.6 6.9 %slice-start.1 = ((s8[6291456]{0:T(1024)(128)(4,1)}), s8[2097152]{0:T(1024)(128)(4,1)S(1)}, s32[]{:S(2)}) async-start(s8[6291456]{0:T(1024)(128)(4,1)} %bitcast.61), calls=%async_computation.4 | async-start | bytes 4194304 | tf_op jit(solution)/shard_map/while
  220.5 6.9 %slice-start = ((s8[6291456]{0:T(1024)(128)(4,1)}), s8[4194304]{0:T(1024)(128)(4,1)S(1)}, s32[]{:S(2)}) async-start(s8[6291456]{0:T(1024)(128)(4,1)} %bitcast.61), calls=%async_computation.3 | async-start | bytes 8388608 | tf_op jit(solution)/shard_map/while
  220.5 6.9 %slice-start.1 = ((s8[6291456]{0:T(1024)(128)(4,1)}), s8[2097152]{0:T(1024)(128)(4,1)S(1)}, s32[]{:S(2)}) async-start(s8[6291456]{0:T(1024)(128)(4,1)} %bitcast.61), calls=%async_computation.4 | async-start | bytes 4194304 | tf_op jit(solution)/shard_map/while
  244.5 6.9 %slice-start = ((s8[6291456]{0:T(1024)(128)(4,1)}), s8[4194304]{0:T(1024)(128)(4,1)S(1)}, s32[]{:S(2)}) async-start(s8[6291456]{0:T(1024)(128)(4,1)} %bitcast.61), calls=%async_computation.3 | async-start | bytes 8388608 | tf_op jit(solution)/shard_map/while
  244.5 6.9 %slice-start.1 = ((s8[6291456]{0:T(1024)(128)(4,1)}), s8[2097152]{0:T(1024)(128)(4,1)S(1)}, s32[]{:S(2)}) async-start(s8[6291456]{0:T(1024)(128)(4,1)} %bitcast.61), calls=%async_computation.4 | async-start | bytes 4194304 | tf_op jit(solution)/shard_map/while
  268.4 6.9 %slice-start = ((s8[6291456]{0:T(1024)(128)(4,1)}), s8[4194304]{0:T(1024)(128)(4,1)S(1)}, s32[]{:S(2)}) async-start(s8[6291456]{0:T(1024)(128)(4,1)} %bitcast.61), calls=%async_computation.3 | async-start | bytes 8388608 | tf_op jit(solution)/shard_map/while
  268.4 6.9 %slice-start.1 = ((s8[6291456]{0:T(1024)(128)(4,1)}), s8[2097152]{0:T(1024)(128)(4,1)S(1)}, s32[]{:S(2)}) async-start(s8[6291456]{0:T(1024)(128)(4,1)} %bitcast.61), calls=%async_computation.4 | async-start | bytes 4194304 | tf_op jit(solution)/shard_map/while
  292.4 6.9 %slice-start = ((s8[6291456]{0:T(1024)(128)(4,1)}), s8[4194304]{0:T(1024)(128)(4,1)S(1)}, s32[]{:S(2)}) async-start(s8[6291456]{0:T(1024)(128)(4,1)} %bitcast.61), calls=%async_computation.3 | async-start | bytes 8388608 | tf_op jit(solution)/shard_map/while
  292.4 6.9 %slice-start.1 = ((s8[6291456]{0:T(1024)(128)(4,1)}), s8[2097152]{0:T(1024)(128)(4,1)S(1)}, s32[]{:S(2)}) async-start(s8[6291456]{0:T(1024)(128)(4,1)} %bitcast.61), calls=%async_computation.4 | async-start | bytes 4194304 | tf_op jit(solution)/shard_map/while
  316.4 6.9 %slice-start = ((s8[6291456]{0:T(1024)(128)(4,1)}), s8[4194304]{0:T(1024)(128)(4,1)S(1)}, s32[]{:S(2)}) async-start(s8[6291456]{0:T(1024)(128)(4,1)} %bitcast.61), calls=%async_computation.3 | async-start | bytes 8388608 | tf_op jit(solution)/shard_map/while
  316.4 6.9 %slice-start.1 = ((s8[6291456]{0:T(1024)(128)(4,1)}), s8[2097152]{0:T(1024)(128)(4,1)S(1)}, s32[]{:S(2)}) async-start(s8[6291456]{0:T(1024)(128)(4,1)} %bitcast.61), calls=%async_computation.4 | async-start | bytes 4194304 | tf_op jit(solution)/shard_map/while
Sparse Core Ops, SparseCore 0:
  344.3 93.5 reduce-scatter.1
